TPU v7x, 32 devices: a whole 2x2x4 slice. The times are simulated.
32 devices in a mesh: seg: 8 (over z, y), ctl: 4 (over x, core).
Axes of the slice: x: 2, y: 2, z: 4, core: 2. Of those that a mesh axis runs over, the one named last changes fastest.
Arguments:
- transition: float32 [8, 1024, 1024], P('seg'), may hold values from -1 to 1
- control_map: float32 [8, 1024, 256], P('seg'), may hold values from -1.5 to 1.5
- weights: float32 [8, 1024], P('seg'), may hold values from 0.01 to 0.5
Outputs:
- sensitivity: float32 [8, 1024, 2048], P('seg', None, 'ctl')
- hessian_tiles: float32 [4, 512, 512], P('ctl', 'seg')
All inputs are finite; a program needn't handle non-finite values.
Results may differ from a plain program's by a relative error of at most 0.0003.
Values sent between devices are 32-bit elements; how exact they have to be, the bound alone decides.
No kernel may reach another device: no remote copies, remote signals or barrier semaphores. Data moves between devices by JAX's collectives and lax.ppermute only.
A program may use at most 128 MiB of HBM per device.

v0:
```python
import jax
import jax.numpy as jnp
from jax import lax
from jax.sharding import PartitionSpec as P


def from_behind(value, axis, by):
    devices = lax.axis_size(axis)
    pairs = [(i, i + by) for i in range(devices) if 0 <= i + by < devices]
    return lax.ppermute(value, axis, pairs)


def matmul_hi(left, right):
    return jnp.dot(left, right, precision=lax.Precision.HIGHEST, preferred_element_type=jnp.float32)


def gather_matrix(m_cols):
    return lax.all_gather(m_cols, "ctl", axis=1, tiled=True)


def earlier_sens(sens_block, reach):
    return from_behind(sens_block, "seg", reach)


def local(transition, control_map, weights):
    own_trans = transition[0]
    own_input = control_map[0]
    weight_row = weights[0]
    nseg = lax.axis_size("seg")
    nctl = lax.axis_size("ctl")
    seg_pos = lax.axis_index("seg")
    ctl_pos = lax.axis_index("ctl")
    stride = nseg // (2 * nctl)
    shard_width = own_trans.shape[1] // nctl
    blocks = [
        jnp.where(seg_pos == (2 * ctl_pos + slot_idx) * stride, own_input, 0.0)
        for slot_idx in range(2)
    ]
    sens_block = jnp.concatenate(blocks, axis=1)
    m_cols = lax.dynamic_slice_in_dim(own_trans, ctl_pos * shard_width, shard_width, 1)
    levels = (nseg - 1).bit_length()
    for level_idx in range(levels):
        reach = 1 << level_idx
        active = seg_pos >= reach
        is_last = level_idx == levels - 1
        own_whole = own_trans if level_idx == 0 else gather_matrix(m_cols)
        if is_last:
            prior_c = earlier_sens(sens_block, reach)
        else:
            prior_m, prior_c = from_behind((m_cols, sens_block), "seg", reach)
            m_cols = jnp.where(active, matmul_hi(own_whole, prior_m), m_cols)
        sens_block = jnp.where(active, matmul_hi(own_whole, prior_c) + sens_block, sens_block)
    weighted = sens_block * weight_row[:, None]
    hess_tile = lax.dot_general(
        sens_block,
        weighted,
        (((0,), (0,)), ((), ())),
        precision=lax.Precision.HIGHEST,
        preferred_element_type=jnp.float32,
    )
    summed = lax.psum(hess_tile, "seg")
    row_count = hess_tile.shape[0] // nseg
    hess_rows = lax.dynamic_slice_in_dim(summed, seg_pos * row_count, row_count, 0)
    return (sens_block[None], hess_rows[None])


def solution(mesh):
    return jax.shard_map(
        local,
        mesh=mesh,
        in_specs=(P("seg", None, None), P("seg", None, None), P("seg", None)),
        out_specs=(P("seg", None, "ctl"), P("ctl", "seg", None)),
        check_vma=False,
    )
```

profile of v0, /device:TPU:0, one launch (start us, length us, event | category | flops | bytes accessed | tf_op | source)
XLA Modules:
  0.0 375.8 jit_solution(13403189669114967752)
XLA Ops:
  7.2 0.0 all-gather.3.cloned.1.call-start
  7.2 1.3 constant_dynamic-slice_fusion
  8.5 0.3 copy.5
  8.9 5.0 %collective-permute-start = (f32[1024,256]{0,1:T(8,128)S(1)}, f32[1024,256]{0,1:T(8,128)S(1)}, u32[]{:S(2)}, u32[]{:S(2)}) collective-permute-start(f32[1024,256]{0,1:T(8,128)S(1)} %bitcast.37), channel_id=1, source_target_pairs={{0,4},{4,8},{8,12},{12,16},{16,20},{20,24},{24,28},{1,5},{5,9},{9,... | collective-permute-start | bytes 3145736 | tf_op jit(solution)/shard_map/ppermute | solution.py:10
  13.8 22.3 %collective-permute-done = f32[1024,256]{0,1:T(8,128)S(1)} collective-permute-done((f32[1024,256]{0,1:T(8,128)S(1)}, f32[1024,256]{0,1:T(8,128)S(1)}, u32[]{:S(2)}, u32[]{:S(2)}) %collective-permute-start) | collective-permute-done | bytes 1048608 | tf_op jit(solution)/shard_map/ppermute | solution.py:10
  36.2 6.9 %fusion.11 = f32[1024,256]{0,1:T(8,128)} fusion(f32[1024,256]{0,1:T(8,128)S(1)} %collective-permute-done, f32[1,1024,1024]{2,1,0:T(8,128)} %param.3, pred[]{:T(512)S(6)} %ge.11, f32[1,1024,256]{1,2,0:T(8,128)S(1)} %copy.5), kind=kOutput, calls=%fused_computation.11 | convolution fusion | flops 3221487616 | bytes 7340033 | tf_op jit(solution)/shard_map/dot_general | solution.py:14
  43.0 0.0 all-gather.3.cloned.1.call-update
  43.1 0.0 all-gather.5.cloned.1.call-start
  43.1 1.3 copy.6
  44.4 6.4 %collective-permute-start.1 = (f32[1024,256]{0,1:T(8,128)S(1)}, f32[1024,256]{0,1:T(8,128)}, u32[]{:S(2)}, u32[]{:S(2)}) collective-permute-start(f32[1024,256]{0,1:T(8,128)S(1)} %copy-done.1), channel_id=1, source_target_pairs={{0,8},{4,12},{8,16},{12,20},{16,24},{20,28},{1,9},{5,13},{9,17},{1... | collective-permute-start | bytes 3145736 | tf_op jit(solution)/shard_map/ppermute | solution.py:10
  50.8 1.6 select_bitcast_fusion.1
  52.4 1.5 pad_maximum_fusion
  53.8 3.8 %collective-permute-start.2 = (f32[1024,512]{0,1:T(8,128)}, f32[1024,512]{0,1:T(8,128)}, u32[]{:S(2)}, u32[]{:S(2)}) collective-permute-start(f32[1024,512]{0,1:T(8,128)} %pad_maximum_fusion), channel_id=1, source_target_pairs={{0,4},{4,8},{8,12},{12,16},{16,20},{20,24},{24,28},{1,5},{5,9},{9,... | collective-permute-start | bytes 6291464 | tf_op jit(solution)/shard_map/ppermute | solution.py:10
  57.6 13.7 %collective-permute-done.1 = f32[1024,256]{0,1:T(8,128)} collective-permute-done((f32[1024,256]{0,1:T(8,128)S(1)}, f32[1024,256]{0,1:T(8,128)}, u32[]{:S(2)}, u32[]{:S(2)}) %collective-permute-start.1) | collective-permute-done | bytes 1048608 | tf_op jit(solution)/shard_map/ppermute | solution.py:10
  71.3 8.6 %all-gather.3.cloned.1.call-done = f32[1024,1024]{0,1:T(8,128)} async-done(((f32[1024,256]{0,1:T(8,128)}), f32[1024,1024]{0,1:T(8,128)}) %all-gather.3.cloned.1.call-update) | async-done | bytes 4194320 | tf_op jit(solution)/shard_map/all_gather | solution.py:18
  79.9 7.3 %convolution_select_fusion = f32[1024,256]{0,1:T(8,128)} fusion(f32[1024,256]{0,1:T(8,128)S(1)} %copy-done.1, f32[1024,1024]{0,1:T(8,128)} %all-gather.3.cloned.1.call-done, f32[1024,256]{0,1:T(8,128)} %collective-permute-done.1, pred[]{:T(512)S(6)} %ge.10), kind=kOutput, calls=%fused_computation.12 | convolution fusion | flops 3221487616 | bytes 7340033 | tf_op jit(solution)/shard_map/dot_general | solution.py:14
  87.1 0.0 all-gather.5.cloned.1.call-update
  87.1 0.2 all-reduce.2.cloned.1.call-start
  87.4 12.9 %collective-permute-done.2 = f32[1024,512]{0,1:T(8,128)} collective-permute-done((f32[1024,512]{0,1:T(8,128)}, f32[1024,512]{0,1:T(8,128)}, u32[]{:S(2)}, u32[]{:S(2)}) %collective-permute-start.2) | collective-permute-done | bytes 2097184 | tf_op jit(solution)/shard_map/ppermute | solution.py:10
  100.3 10.0 %add_select_fusion.2 = f32[1024,512]{0,1:T(8,128)S(1)} fusion(f32[1024,512]{0,1:T(8,128)} %collective-permute-done.2, f32[1,1024,1024]{2,1,0:T(8,128)} %param.3, pred[]{:T(512)S(6)} %ge.11, f32[1024,256]{0,1:T(8,128)S(1)} %get-tuple-element.5, f32[1024,256]{0,1:T(8,128)S(1)} %get-tuple-element.4), kind=kOutput, calls=%fused_computation.8 | convolution fusion | flops 6444023808 | bytes 10485761 | tf_op jit(solution)/shard_map/dot_general | solution.py:14
  110.3 20.6 %collective-permute-start.3 = (f32[1024,512]{0,1:T(8,128)S(1)}, f32[1024,512]{0,1:T(8,128)S(1)}, u32[]{:S(2)}, u32[]{:S(2)}) collective-permute-start(f32[1024,512]{0,1:T(8,128)S(1)} %add_select_fusion.2), channel_id=1, source_target_pairs={{0,8},{4,12},{8,16},{12,20},{16,24},{20,28},{1,9},{5,13},{9,17},{1... | collective-permute-start | bytes 6291464 | tf_op jit(solution)/shard_map/ppermute | solution.py:10
  131.0 43.0 %collective-permute-done.3 = f32[1024,512]{0,1:T(8,128)S(1)} collective-permute-done((f32[1024,512]{0,1:T(8,128)S(1)}, f32[1024,512]{0,1:T(8,128)S(1)}, u32[]{:S(2)}, u32[]{:S(2)}) %collective-permute-start.3) | collective-permute-done | bytes 2097184 | tf_op jit(solution)/shard_map/ppermute | solution.py:10
  174.0 7.0 %add_select_fusion.1 = f32[1024,512]{0,1:T(8,128)S(1)} fusion(f32[1024,512]{0,1:T(8,128)S(1)} %add_select_fusion.2, f32[1024,1024]{0,1:T(8,128)S(1)} %copy-done, f32[1024,512]{0,1:T(8,128)S(1)} %collective-permute-done.3, pred[]{:T(512)S(6)} %ge.10), kind=kOutput, calls=%fused_computation.7 | convolution fusion | flops 6443499520 | bytes 10485761 | tf_op jit(solution)/shard_map/dot_general | solution.py:14
  180.9 0.0 copy-start.2
  180.9 6.8 %collective-permute-start.4 = (f32[1024,512]{0,1:T(8,128)S(1)}, f32[1024,512]{0,1:T(8,128)}, u32[]{:S(2)}, u32[]{:S(2)}) collective-permute-start(f32[1024,512]{0,1:T(8,128)S(1)} %add_select_fusion.1), channel_id=1, source_target_pairs={{0,16},{4,20},{8,24},{12,28},{1,17},{5,21},{9,25},{13,29},{2,18},{... | collective-permute-start | bytes 6291464 | tf_op jit(solution)/shard_map/ppermute | solution.py:10
  187.7 41.0 %collective-permute-done.4 = f32[1024,512]{0,1:T(8,128)} collective-permute-done((f32[1024,512]{0,1:T(8,128)S(1)}, f32[1024,512]{0,1:T(8,128)}, u32[]{:S(2)}, u32[]{:S(2)}) %collective-permute-start.4) | collective-permute-done | bytes 2097184 | tf_op jit(solution)/shard_map/ppermute | solution.py:10
  228.7 9.8 %add_select_fusion = f32[1024,512]{0,1:T(8,128)S(1)} fusion(f32[1024,512]{0,1:T(8,128)} %copy-done.2, f32[1024,1024]{0,1:T(8,128)} %all-gather.5.cloned.1.call-done, f32[1024,512]{0,1:T(8,128)} %collective-permute-done.4, pred[]{:T(512)S(6)} %ge.9), kind=kOutput, calls=%fused_computation.6 | convolution fusion | flops 6443499520 | bytes 10485761 | tf_op jit(solution)/shard_map/dot_general | solution.py:14
  238.5 4.5 %fusion.4 = f32[512,512]{1,0:T(8,128)} fusion(f32[1024,512]{0,1:T(8,128)S(1)} %add_select_fusion, f32[1024]{0:T(1024)S(1)} %bitcast.38), kind=kOutput, calls=%fused_computation.4 | convolution fusion | flops 3221749760 | bytes 3149824 | tf_op jit(solution)/shard_map/dot_general | solution.py:54
  243.1 0.0 all-reduce.2.cloned.1.call-update
  243.1 1.8 copy.10
  244.9 122.8 %all-reduce.2.cloned.1.call-done = f32[512,512]{1,0:T(8,128)} async-done(((f32[512,512]{1,0:T(8,128)}), f32[512,512]{1,0:T(8,128)}) %all-reduce.2.cloned.1.call-update) | async-done | bytes 1048592 | tf_op jit(solution)/shard_map/psum | solution.py:61
  367.7 1.6 dynamic-slice_bitcast_fusion
  (10 shorter events, 0.0 us)
Async XLA Ops:
  7.2 72.7 %all-gather.3.cloned.1.call-start = ((), (), s32[]{:S(2)}) async-start(), calls=%async_computation | async-start | bytes 5242880 | tf_op jit(solution)/shard_map/all_gather | solution.py:18
  8.9 27.3 %collective-permute-start = (f32[1024,256]{0,1:T(8,128)S(1)}, f32[1024,256]{0,1:T(8,128)S(1)}, u32[]{:S(2)}, u32[]{:S(2)}) collective-permute-start(f32[1024,256]{0,1:T(8,128)S(1)} %bitcast.37), channel_id=1, source_target_pairs={{0,4},{4,8},{8,12},{12,16},{16,20},{20,24},{24,28},{1,5},{5,9},{9,... | collective-permute-start | bytes 3145736 | tf_op jit(solution)/shard_map/ppermute | solution.py:10
  13.8 29.3 %copy-start.3 = (f32[1,1024,256]{2,1,0:T(8,128)S(1)}, f32[1,1024,256]{2,1,0:T(8,128)}, u32[]{:S(2)}) copy-start(f32[1,1024,256]{2,1,0:T(8,128)} %param.4) | copy-start | bytes 3145732
  43.0 1.4 copy-start.1
  43.1 185.6 %all-gather.5.cloned.1.call-start = ((), (), s32[]{:S(2)}) async-start(), calls=%async_computation.1 | async-start | bytes 5242880 | tf_op jit(solution)/shard_map/all_gather | solution.py:18
  44.4 26.9 %collective-permute-start.1 = (f32[1024,256]{0,1:T(8,128)S(1)}, f32[1024,256]{0,1:T(8,128)}, u32[]{:S(2)}, u32[]{:S(2)}) collective-permute-start(f32[1024,256]{0,1:T(8,128)S(1)} %copy-done.1), channel_id=1, source_target_pairs={{0,8},{4,12},{8,16},{12,20},{16,24},{20,28},{1,9},{5,13},{9,17},{1... | collective-permute-start | bytes 3145736 | tf_op jit(solution)/shard_map/ppermute | solution.py:10
  53.8 46.5 %collective-permute-start.2 = (f32[1024,512]{0,1:T(8,128)}, f32[1024,512]{0,1:T(8,128)}, u32[]{:S(2)}, u32[]{:S(2)}) collective-permute-start(f32[1024,512]{0,1:T(8,128)} %pad_maximum_fusion), channel_id=1, source_target_pairs={{0,4},{4,8},{8,12},{12,16},{16,20},{20,24},{24,28},{1,5},{5,9},{9,... | collective-permute-start | bytes 6291464 | tf_op jit(solution)/shard_map/ppermute | solution.py:10
  87.1 280.6 %all-reduce.2.cloned.1.call-start = ((), (), s32[]{:S(2)}) async-start(), calls=%async_computation.2 | async-start | bytes 2097152 | tf_op jit(solution)/shard_map/psum | solution.py:61
  100.3 73.7 %copy-start = (f32[1024,1024]{0,1:T(8,128)S(1)}, f32[1024,1024]{0,1:T(8,128)}, u32[]{:S(2)}) copy-start(f32[1024,1024]{0,1:T(8,128)} %all-gather.3.cloned.1.call-done) | copy-start | bytes 12582916
  110.3 63.6 %collective-permute-start.3 = (f32[1024,512]{0,1:T(8,128)S(1)}, f32[1024,512]{0,1:T(8,128)S(1)}, u32[]{:S(2)}, u32[]{:S(2)}) collective-permute-start(f32[1024,512]{0,1:T(8,128)S(1)} %add_select_fusion.2), channel_id=1, source_target_pairs={{0,8},{4,12},{8,16},{12,20},{16,24},{20,28},{1,9},{5,13},{9,17},{1... | collective-permute-start | bytes 6291464 | tf_op jit(solution)/shard_map/ppermute | solution.py:10
  180.9 47.7 %copy-start.2 = (f32[1024,512]{0,1:T(8,128)}, f32[1024,512]{0,1:T(8,128)S(1)}, u32[]{:S(2)}) copy-start(f32[1024,512]{0,1:T(8,128)S(1)} %add_select_fusion.1) | copy-start | bytes 6291460
  180.9 47.7 %collective-permute-start.4 = (f32[1024,512]{0,1:T(8,128)S(1)}, f32[1024,512]{0,1:T(8,128)}, u32[]{:S(2)}, u32[]{:S(2)}) collective-permute-start(f32[1024,512]{0,1:T(8,128)S(1)} %add_select_fusion.1), channel_id=1, source_target_pairs={{0,16},{4,20},{8,24},{12,28},{1,17},{5,21},{9,25},{13,29},{2,18},{... | collective-permute-start | bytes 6291464 | tf_op jit(solution)/shard_map/ppermute | solution.py:10
  187.7 50.8 %copy-start.4 = (f32[1,1024]{1,0:T(1,128)S(1)}, f32[1,1024]{1,0:T(1,128)}, u32[]{:S(2)}) copy-start(f32[1,1024]{1,0:T(1,128)} %param.5) | copy-start | bytes 12292
Sparse Core Ops, SparseCore 0:
  43.2 36.6 all-gather.2
  87.3 34.4 all-gather.4
  243.2 124.4 all-reduce.1
where the time goes:
time: 376 us
  waiting for transfers between devices  264 us (70%)
  matrix products  45.5 us (12%)
  starting transfers between devices  42.8 us (11%)
  between operations  13.9 us (4%)
  local copies, waits for them, and re-layouts  6.34 us (2%)
    ppermute x5, waiting for transfers between devices, from_behind(): return lax.ppermute(value, axis, pairs)  133 us
    psum x1, waiting for transfers between devices, local(): summed = lax.psum(hess_tile, 'seg')  123 us
    ppermute x5, starting transfers between devices, from_behind(): return lax.ppermute(value, axis, pairs)  42.5 us
    dot_general x5, matrix products, matmul_hi(): jnp.dot(left, right, precision=lax.Precision.HIGHEST, preferred_element_t...  40.9 us
    all_gather x2, waiting for transfers between devices, gather_matrix(): return lax.all_gather(m_cols, 'ctl', axis=1, tiled=True)  8.56 us
  transfers between devices with their start and end apart: 8, of which 7 were waited for; matrix products, arithmetic and copies ran while one was open for 8% of the time, Pallas kernels for 0%

commit v1 on v0

--- a/solution.py
+++ b/solution.py
@@ -1,7 +1,21 @@
+import functools
 import jax
 import jax.numpy as jnp
 from jax import lax
 from jax.sharding import PartitionSpec as P
+
+
+def _connect_run(t0, across):
+    cores_n = lax.axis_size(across)
+    earlier, latest = (t0, 0)
+    while 1 << latest < cores_n:
+        formed = lax.ppermute(earlier, across, [(u, u ^ 1 << latest) for u in range(cores_n)])
+        earlier = earlier + formed
+        latest = latest + 1
+    return earlier
+
+
+advance_the_levels_all = functools.partial(_connect_run, across="seg")
 
 
 def from_behind(value, axis, by):
@@ -58,7 +72,7 @@
         precision=lax.Precision.HIGHEST,
         preferred_element_type=jnp.float32,
     )
-    summed = lax.psum(hess_tile, "seg")
+    summed = advance_the_levels_all(hess_tile)
     row_count = hess_tile.shape[0] // nseg
     hess_rows = lax.dynamic_slice_in_dim(summed, seg_pos * row_count, row_count, 0)
     return (sens_block[None], hess_rows[None])

time: 376 us -> 393 us (1.045)
  starting transfers between devices: 42.8 us -> 96.5 us
  waiting for transfers between devices: 264 us -> 228 us
    psum x1 -> x0, waiting for transfers between devices: 123 us -> none  [local(): summed = lax.psum(hess_tile, 'seg')]
    ppermute x0 -> x3, waiting for transfers between devices: none -> 86.6 us  [_connect_run(): lax.ppermute(earlier, across, [(u, u ^ 1 << latest) for u in range(cores_...]
    ppermute x0 -> x3, starting transfers between devices: none -> 53.7 us  [_connect_run(): lax.ppermute(earlier, across, [(u, u ^ 1 << latest) for u in range(cores_...]
  transfers between devices with their start and end apart: 8 -> 10, of which waited for: 7 -> 9; matrix products, arithmetic and copies ran while one was open for 8% -> 8% of each run, Pallas kernels for 0% -> 0%
where the time goes in v1:
time: 393 us
  waiting for transfers between devices  228 us (58%)
  starting transfers between devices  96.5 us (25%)
  matrix products  44.5 us (11%)
  between operations  14.2 us (4%)
  other arithmetic  5.02 us (1%)
  local copies, waits for them, and re-layouts  4.76 us (1%)
    ppermute x5, waiting for transfers between devices, from_behind(): return lax.ppermute(value, axis, pairs)  133 us
    ppermute x3, waiting for transfers between devices, _connect_run(): lax.ppermute(earlier, across, [(u, u ^ 1 << latest) for u in range(cores_...  86.6 us
    ppermute x3, starting transfers between devices, _connect_run(): lax.ppermute(earlier, across, [(u, u ^ 1 << latest) for u in range(cores_...  53.7 us
    ppermute x5, starting transfers between devices, from_behind(): return lax.ppermute(value, axis, pairs)  42.7 us
    dot_general x5, matrix products, matmul_hi(): jnp.dot(left, right, precision=lax.Precision.HIGHEST, preferred_element_t...  40.9 us
    all_gather x2, waiting for transfers between devices, gather_matrix(): return lax.all_gather(m_cols, 'ctl', axis=1, tiled=True)  8.56 us
  transfers between devices with their start and end apart: 10, of which 9 were waited for; matrix products, arithmetic and copies ran while one was open for 8% of the time, Pallas kernels for 0%

profile of v1, /device:TPU:0, one launch (start us, length us, event | category | flops | bytes accessed | tf_op | source)
XLA Modules:
  0.0 393.0 jit_solution(2678284901564741933)
XLA Ops:
  7.2 1.3 constant_dynamic-slice_fusion
  8.5 0.3 copy.5
  8.9 5.0 %collective-permute-start = (f32[1024,256]{0,1:T(8,128)S(1)}, f32[1024,256]{0,1:T(8,128)S(1)}, u32[]{:S(2)}, u32[]{:S(2)}) collective-permute-start(f32[1024,256]{0,1:T(8,128)S(1)} %bitcast.37), channel_id=1, source_target_pairs={{0,4},{4,8},{8,12},{12,16},{16,20},{20,24},{24,28},{1,5},{5,9},{9,... | collective-permute-start | bytes 3145736 | tf_op jit(solution)/shard_map/ppermute | solution.py:24
  13.8 22.3 %collective-permute-done = f32[1024,256]{0,1:T(8,128)S(1)} collective-permute-done((f32[1024,256]{0,1:T(8,128)S(1)}, f32[1024,256]{0,1:T(8,128)S(1)}, u32[]{:S(2)}, u32[]{:S(2)}) %collective-permute-start) | collective-permute-done | bytes 1048608 | tf_op jit(solution)/shard_map/ppermute | solution.py:24
  36.2 6.9 %fusion.11 = f32[1024,256]{0,1:T(8,128)} fusion(f32[1024,256]{0,1:T(8,128)S(1)} %collective-permute-done, f32[1,1024,1024]{2,1,0:T(8,128)} %param.3, pred[]{:T(512)S(6)} %ge.11, f32[1,1024,256]{1,2,0:T(8,128)S(1)} %copy.5), kind=kOutput, calls=%fused_computation.11 | convolution fusion | flops 3221487616 | bytes 7340033 | tf_op jit(solution)/shard_map/dot_general | solution.py:28
  43.1 1.3 copy.6
  44.4 6.3 %collective-permute-start.1 = (f32[1024,256]{0,1:T(8,128)S(1)}, f32[1024,256]{0,1:T(8,128)}, u32[]{:S(2)}, u32[]{:S(2)}) collective-permute-start(f32[1024,256]{0,1:T(8,128)S(1)} %copy-done.1), channel_id=1, source_target_pairs={{0,8},{4,12},{8,16},{12,20},{16,24},{20,28},{1,9},{5,13},{9,17},{1... | collective-permute-start | bytes 3145736 | tf_op jit(solution)/shard_map/ppermute | solution.py:24
  50.8 1.6 select_bitcast_fusion.1
  52.3 1.5 pad_maximum_fusion
  53.8 3.8 collective-permute-start.2
  57.6 13.7 %collective-permute-done.1 = f32[1024,256]{0,1:T(8,128)} collective-permute-done((f32[1024,256]{0,1:T(8,128)S(1)}, f32[1024,256]{0,1:T(8,128)}, u32[]{:S(2)}, u32[]{:S(2)}) %collective-permute-start.1) | collective-permute-done | bytes 1048608 | tf_op jit(solution)/shard_map/ppermute | solution.py:24
  71.3 8.6 %all-gather.3.cloned.1.call-done = f32[1024,1024]{0,1:T(8,128)} async-done(((f32[1024,256]{0,1:T(8,128)}), f32[1024,1024]{0,1:T(8,128)}) %all-gather.3.cloned.1.call-update) | async-done | bytes 4194320 | tf_op jit(solution)/shard_map/all_gather | solution.py:32
  79.9 7.2 %convolution_select_fusion = f32[1024,256]{0,1:T(8,128)} fusion(f32[1024,256]{0,1:T(8,128)S(1)} %copy-done.1, f32[1024,1024]{0,1:T(8,128)} %all-gather.3.cloned.1.call-done, f32[1024,256]{0,1:T(8,128)} %collective-permute-done.1, pred[]{:T(512)S(6)} %ge.10), kind=kOutput, calls=%fused_computation.12 | convolution fusion | flops 3221487616 | bytes 7340033 | tf_op jit(solution)/shard_map/dot_general | solution.py:28
  87.1 13.2 %collective-permute-done.2 = f32[1024,512]{0,1:T(8,128)} collective-permute-done((f32[1024,512]{0,1:T(8,128)}, f32[1024,512]{0,1:T(8,128)}, u32[]{:S(2)}, u32[]{:S(2)}) %collective-permute-start.2) | collective-permute-done | bytes 2097184 | tf_op jit(solution)/shard_map/ppermute | solution.py:24
  100.3 10.0 %add_select_fusion.2 = f32[1024,512]{0,1:T(8,128)S(1)} fusion(f32[1024,512]{0,1:T(8,128)} %collective-permute-done.2, f32[1,1024,1024]{2,1,0:T(8,128)} %param.3, pred[]{:T(512)S(6)} %ge.11, f32[1024,256]{0,1:T(8,128)S(1)} %get-tuple-element.5, f32[1024,256]{0,1:T(8,128)S(1)} %get-tuple-element.4), kind=kOutput, calls=%fused_computation.8 | convolution fusion | flops 6444023808 | bytes 10485761 | tf_op jit(solution)/shard_map/dot_general | solution.py:28
  110.3 20.9 %collective-permute-start.3 = (f32[1024,512]{0,1:T(8,128)S(1)}, f32[1024,512]{0,1:T(8,128)S(1)}, u32[]{:S(2)}, u32[]{:S(2)}) collective-permute-start(f32[1024,512]{0,1:T(8,128)S(1)} %add_select_fusion.2), channel_id=1, source_target_pairs={{0,8},{4,12},{8,16},{12,20},{16,24},{20,28},{1,9},{5,13},{9,17},{1... | collective-permute-start | bytes 6291464 | tf_op jit(solution)/shard_map/ppermute | solution.py:24
  131.2 42.8 %collective-permute-done.3 = f32[1024,512]{0,1:T(8,128)S(1)} collective-permute-done((f32[1024,512]{0,1:T(8,128)S(1)}, f32[1024,512]{0,1:T(8,128)S(1)}, u32[]{:S(2)}, u32[]{:S(2)}) %collective-permute-start.3) | collective-permute-done | bytes 2097184 | tf_op jit(solution)/shard_map/ppermute | solution.py:24
  174.0 7.0 %add_select_fusion.1 = f32[1024,512]{0,1:T(8,128)S(1)} fusion(f32[1024,512]{0,1:T(8,128)S(1)} %add_select_fusion.2, f32[1024,1024]{0,1:T(8,128)S(1)} %copy-done, f32[1024,512]{0,1:T(8,128)S(1)} %collective-permute-done.3, pred[]{:T(512)S(6)} %ge.10), kind=kOutput, calls=%fused_computation.7 | convolution fusion | flops 6443499520 | bytes 10485761 | tf_op jit(solution)/shard_map/dot_general | solution.py:28
  180.9 6.7 %collective-permute-start.4 = (f32[1024,512]{0,1:T(8,128)S(1)}, f32[1024,512]{0,1:T(8,128)}, u32[]{:S(2)}, u32[]{:S(2)}) collective-permute-start(f32[1024,512]{0,1:T(8,128)S(1)} %add_select_fusion.1), channel_id=1, source_target_pairs={{0,16},{4,20},{8,24},{12,28},{1,17},{5,21},{9,25},{13,29},{2,18},{... | collective-permute-start | bytes 6291464 | tf_op jit(solution)/shard_map/ppermute | solution.py:24
  187.7 41.0 %collective-permute-done.4 = f32[1024,512]{0,1:T(8,128)} collective-permute-done((f32[1024,512]{0,1:T(8,128)S(1)}, f32[1024,512]{0,1:T(8,128)}, u32[]{:S(2)}, u32[]{:S(2)}) %collective-permute-start.4) | collective-permute-done | bytes 2097184 | tf_op jit(solution)/shard_map/ppermute | solution.py:24
  228.7 9.8 %add_select_fusion = f32[1024,512]{0,1:T(8,128)S(1)} fusion(f32[1024,512]{0,1:T(8,128)} %copy-done.2, f32[1024,1024]{0,1:T(8,128)} %all-gather.5.cloned.1.call-done, f32[1024,512]{0,1:T(8,128)} %collective-permute-done.4, pred[]{:T(512)S(6)} %ge.9), kind=kOutput, calls=%fused_computation.6 | convolution fusion | flops 6443499520 | bytes 10485761 | tf_op jit(solution)/shard_map/dot_general | solution.py:28
  238.5 3.5 fusion.4
  242.1 0.1 collective-permute-start.5
  242.1 21.5 %collective-permute-done.5 = f32[512,512]{1,0:T(8,128)S(1)} collective-permute-done((f32[512,512]{1,0:T(8,128)S(1)}, f32[512,512]{1,0:T(8,128)S(1)}, u32[]{:S(2)}, u32[]{:S(2)}) %collective-permute-start.5) | collective-permute-done | bytes 1048608 | tf_op jit(solution)/shard_map/ppermute | solution.py:12
  263.6 0.2 add.32
  263.8 50.0 %collective-permute-start.6 = (f32[512,512]{1,0:T(8,128)S(1)}, f32[512,512]{1,0:T(8,128)S(1)}, u32[]{:S(2)}, u32[]{:S(2)}) collective-permute-start(f32[512,512]{1,0:T(8,128)S(1)} %add.32), channel_id=1, source_target_pairs={{0,8},{4,12},{8,0},{12,4},{16,24},{20,28},{24,16},{28,20},{1,9},{5... | collective-permute-start | bytes 3145736 | tf_op jit(solution)/shard_map/ppermute | solution.py:12
  313.8 22.5 %collective-permute-done.6 = f32[512,512]{1,0:T(8,128)S(1)} collective-permute-done((f32[512,512]{1,0:T(8,128)S(1)}, f32[512,512]{1,0:T(8,128)S(1)}, u32[]{:S(2)}, u32[]{:S(2)}) %collective-permute-start.6) | collective-permute-done | bytes 1048608 | tf_op jit(solution)/shard_map/ppermute | solution.py:12
  336.3 0.2 add.33
  336.5 3.6 collective-permute-start.7
  340.1 1.8 copy.10
  341.9 42.7 %collective-permute-done.7 = f32[512,512]{1,0:T(8,128)} collective-permute-done((f32[512,512]{1,0:T(8,128)S(1)}, f32[512,512]{1,0:T(8,128)}, u32[]{:S(2)}, u32[]{:S(2)}) %collective-permute-start.7) | collective-permute-done | bytes 1048608 | tf_op jit(solution)/shard_map/ppermute | solution.py:12
  384.6 1.6 fusion.15
  (15 shorter events, 0.1 us)
Async XLA Ops:
  7.2 72.7 %all-gather.3.cloned.1.call-start = ((), (), s32[]{:S(2)}) async-start(), calls=%async_computation | async-start | bytes 5242880 | tf_op jit(solution)/shard_map/all_gather | solution.py:32
  8.9 27.3 %collective-permute-start = (f32[1024,256]{0,1:T(8,128)S(1)}, f32[1024,256]{0,1:T(8,128)S(1)}, u32[]{:S(2)}, u32[]{:S(2)}) collective-permute-start(f32[1024,256]{0,1:T(8,128)S(1)} %bitcast.37), channel_id=1, source_target_pairs={{0,4},{4,8},{8,12},{12,16},{16,20},{20,24},{24,28},{1,5},{5,9},{9,... | collective-permute-start | bytes 3145736 | tf_op jit(solution)/shard_map/ppermute | solution.py:24
  13.8 29.3 %copy-start.3 = (f32[1,1024,256]{2,1,0:T(8,128)S(1)}, f32[1,1024,256]{2,1,0:T(8,128)}, u32[]{:S(2)}) copy-start(f32[1,1024,256]{2,1,0:T(8,128)} %param.4) | copy-start | bytes 3145732
  43.0 1.4 copy-start.1
  43.0 185.6 %all-gather.5.cloned.1.call-start = ((), (), s32[]{:S(2)}) async-start(), calls=%async_computation.1 | async-start | bytes 5242880 | tf_op jit(solution)/shard_map/all_gather | solution.py:32
  44.4 26.9 %collective-permute-start.1 = (f32[1024,256]{0,1:T(8,128)S(1)}, f32[1024,256]{0,1:T(8,128)}, u32[]{:S(2)}, u32[]{:S(2)}) collective-permute-start(f32[1024,256]{0,1:T(8,128)S(1)} %copy-done.1), channel_id=1, source_target_pairs={{0,8},{4,12},{8,16},{12,20},{16,24},{20,28},{1,9},{5,13},{9,17},{1... | collective-permute-start | bytes 3145736 | tf_op jit(solution)/shard_map/ppermute | solution.py:24
  53.8 46.5 %collective-permute-start.2 = (f32[1024,512]{0,1:T(8,128)}, f32[1024,512]{0,1:T(8,128)}, u32[]{:S(2)}, u32[]{:S(2)}) collective-permute-start(f32[1024,512]{0,1:T(8,128)} %pad_maximum_fusion), channel_id=1, source_target_pairs={{0,4},{4,8},{8,12},{12,16},{16,20},{20,24},{24,28},{1,5},{5,9},{9,... | collective-permute-start | bytes 6291464 | tf_op jit(solution)/shard_map/ppermute | solution.py:24
  100.3 73.7 %copy-start = (f32[1024,1024]{0,1:T(8,128)S(1)}, f32[1024,1024]{0,1:T(8,128)}, u32[]{:S(2)}) copy-start(f32[1024,1024]{0,1:T(8,128)} %all-gather.3.cloned.1.call-done) | copy-start | bytes 12582916
  110.3 63.6 %collective-permute-start.3 = (f32[1024,512]{0,1:T(8,128)S(1)}, f32[1024,512]{0,1:T(8,128)S(1)}, u32[]{:S(2)}, u32[]{:S(2)}) collective-permute-start(f32[1024,512]{0,1:T(8,128)S(1)} %add_select_fusion.2), channel_id=1, source_target_pairs={{0,8},{4,12},{8,16},{12,20},{16,24},{20,28},{1,9},{5,13},{9,17},{1... | collective-permute-start | bytes 6291464 | tf_op jit(solution)/shard_map/ppermute | solution.py:24
  180.9 47.7 %copy-start.2 = (f32[1024,512]{0,1:T(8,128)}, f32[1024,512]{0,1:T(8,128)S(1)}, u32[]{:S(2)}) copy-start(f32[1024,512]{0,1:T(8,128)S(1)} %add_select_fusion.1) | copy-start | bytes 6291460
  180.9 47.7 %collective-permute-start.4 = (f32[1024,512]{0,1:T(8,128)S(1)}, f32[1024,512]{0,1:T(8,128)}, u32[]{:S(2)}, u32[]{:S(2)}) collective-permute-start(f32[1024,512]{0,1:T(8,128)S(1)} %add_select_fusion.1), channel_id=1, source_target_pairs={{0,16},{4,20},{8,24},{12,28},{1,17},{5,21},{9,25},{13,29},{2,18},{... | collective-permute-start | bytes 6291464 | tf_op jit(solution)/shard_map/ppermute | solution.py:24
  187.7 50.8 %copy-start.4 = (f32[1,1024]{1,0:T(1,128)S(1)}, f32[1,1024]{1,0:T(1,128)}, u32[]{:S(2)}) copy-start(f32[1,1024]{1,0:T(1,128)} %param.5) | copy-start | bytes 12292
  242.1 21.5 %collective-permute-start.5 = (f32[512,512]{1,0:T(8,128)S(1)}, f32[512,512]{1,0:T(8,128)S(1)}, u32[]{:S(2)}, u32[]{:S(2)}) collective-permute-start(f32[512,512]{1,0:T(8,128)S(1)} %fusion.4), channel_id=1, source_target_pairs={{0,4},{4,0},{8,12},{12,8},{16,20},{20,16},{24,28},{28,24},{1,5},{5... | collective-permute-start | bytes 3145736 | tf_op jit(solution)/shard_map/ppermute | solution.py:12
  263.8 72.5 %collective-permute-start.6 = (f32[512,512]{1,0:T(8,128)S(1)}, f32[512,512]{1,0:T(8,128)S(1)}, u32[]{:S(2)}, u32[]{:S(2)}) collective-permute-start(f32[512,512]{1,0:T(8,128)S(1)} %add.32), channel_id=1, source_target_pairs={{0,8},{4,12},{8,0},{12,4},{16,24},{20,28},{24,16},{28,20},{1,9},{5... | collective-permute-start | bytes 3145736 | tf_op jit(solution)/shard_map/ppermute | solution.py:12
  336.5 48.0 %collective-permute-start.7 = (f32[512,512]{1,0:T(8,128)S(1)}, f32[512,512]{1,0:T(8,128)}, u32[]{:S(2)}, u32[]{:S(2)}) collective-permute-start(f32[512,512]{1,0:T(8,128)S(1)} %add.33), channel_id=1, source_target_pairs={{0,16},{4,20},{8,24},{12,28},{16,0},{20,4},{24,8},{28,12},{1,17},{... | collective-permute-start | bytes 3145736 | tf_op jit(solution)/shard_map/ppermute | solution.py:12
Sparse Core Ops, SparseCore 0:
  43.2 36.6 all-gather.2
  87.2 34.4 all-gather.4
